TPU v7x, 32 devices: a whole 2x2x4 slice. The times are simulated.
32 devices in a mesh: occ: 4 (over z), va: 2 (over x), vb: 4 (over y, core).
Axes of the slice: x: 2, y: 2, z: 4, core: 2. Of those that a mesh axis runs over, the one named last changes fastest.
Arguments:
- aux_factors: bfloat16 [4, 1024, 2048], P('occ', ('vb', 'va')), may hold values from -0.59765625 to 0.59765625
- occ_energy: float32 [4], replicated, may hold values from -2 to -0.5
- vir_energy: float32 [1024], replicated, may hold values from 0.5 to 3
- occ_index: int32 [4], replicated, may hold values from 0 to 3, each once
- vir_index: int32 [1024], replicated, may hold values from 0 to 1023, each once
Outputs:
- gamma_aux: float32 [4, 1024, 2048], P('occ', ('vb', 'va'))
Inputs may be any that keep to these rules, and one draw needn't show every extreme that they name: `occ_index`: each occupied table row appears exactly once. `vir_index`: each virtual table row appears exactly once.
All inputs are finite; a program needn't handle non-finite values.
Results may differ from a plain program's by a relative error of at most 0.0017.
Values may be sent and summed in bfloat16 or wider, within the bound.
No kernel may reach another device: no remote copies, remote signals or barrier semaphores. Data moves between devices by JAX's collectives and lax.ppermute only.
A program may use at most 64 MiB of HBM per device.

v0:
```python
import jax
import jax.numpy as jnp
from jax import lax
from jax.sharding import PartitionSpec as P

STEPS = 4


def passed_along(block, axis, distance):
    devices = range(lax.axis_size(axis))
    route = [((i - distance) % len(devices), i) for i in devices]
    return lax.ppermute(block, axis, route)


def lookup(indices, energies):
    positions = jnp.arange(energies.shape[0], dtype=jnp.int32)
    matches = indices[:, None] == positions[None, :]
    return jnp.sum(jnp.where(matches, energies[None, :], 0.0), axis=1)


def per_device(aux_factors, occ_energy, vir_energy, occ_index, vir_index):
    va_count = lax.axis_size("va")
    vb_count = lax.axis_size("vb")
    occ_count = lax.axis_size("occ")
    va_rank = lax.axis_index("va")
    vb_rank = lax.axis_index("vb")
    occ_rank = lax.axis_index("occ")
    occ_rows, block_width, aux_width = aux_factors.shape
    vir_width = vir_index.shape[0]
    row_count = vb_count * block_width
    col_count = va_count * block_width
    row_index = lax.dynamic_index_in_dim(
        vir_index.reshape(vb_count, va_count, block_width), va_rank, 1, False
    ).reshape(row_count)
    col_index = lax.dynamic_index_in_dim(
        vir_index.reshape(vb_count, vir_width // vb_count), vb_rank, 0, False
    )
    row_energy = lookup(row_index, vir_energy)
    col_energy = lookup(col_index, vir_energy)

    def block_energy(block_id):
        return lookup(
            lax.dynamic_slice_in_dim(occ_index, block_id * occ_rows, occ_rows), occ_energy
        )

    own_energy = block_energy(occ_rank)
    own_columns = lax.all_gather(aux_factors, "va", axis=1, tiled=True)
    own_rows = lax.all_gather(aux_factors, "vb", axis=1, tiled=True)
    gradient = jnp.zeros((occ_rows, row_count, aux_width), jnp.float32)
    far_columns = own_columns
    for distance in range(STEPS):
        if distance > 0:
            far_columns = passed_along(far_columns, "occ", 1)
        far_block = (occ_rank - distance + occ_count) % occ_count
        kernel = jnp.einsum(
            "iap,jbp->iajb", own_rows, far_columns, preferred_element_type=jnp.float32
        )
        outgoing = kernel.reshape(occ_rows, vb_count, block_width, occ_rows, va_count, block_width)
        outgoing = outgoing.transpose(4, 1, 0, 2, 3, 5).reshape(
            va_count * vb_count, occ_rows, block_width, occ_rows, block_width
        )
        incoming = lax.all_to_all(outgoing, ("va", "vb"), split_axis=0, concat_axis=0, tiled=True)
        incoming = incoming.reshape(
            va_count, vb_count, occ_rows, block_width, occ_rows, block_width
        )
        swapped = incoming.transpose(2, 1, 5, 4, 0, 3).reshape(
            occ_rows, row_count, occ_rows, col_count
        )
        energy_gap = (
            own_energy[:, None, None, None]
            + block_energy(far_block)[None, None, :, None]
            - row_energy[None, :, None, None]
            - col_energy[None, None, None, :]
        )
        weights = ((2.0 * kernel - swapped) / energy_gap).astype(jnp.bfloat16)
        gradient = gradient + jnp.einsum(
            "iajb,jbp->iap", weights, far_columns, preferred_element_type=jnp.float32
        )
    return lax.psum_scatter(gradient, "vb", scatter_dimension=1, tiled=True)


def solution(mesh):
    return jax.shard_map(
        per_device,
        mesh=mesh,
        in_specs=(P("occ", ("vb", "va"), None), P(), P(), P(), P()),
        out_specs=P("occ", ("vb", "va"), None),
        check_vma=False,
    )
```

profile of v0, /device:TPU:0, one launch (start us, length us, event | category | flops | bytes accessed | tf_op | source)
XLA Modules:
  0.0 195.6 jit_solution(13095508665357366006)
XLA Ops:
  6.5 0.0 all-gather.5.cloned.1.call-start
  6.5 0.7 all-gather.5.cloned.1.call-update
  7.3 0.0 all-gather.3.cloned.1.call-start
  7.3 0.7 all-gather.3.cloned.1.call-update
  8.0 24.9 %all-gather.5.cloned.1.call-done = bf16[1,256,2048]{2,1,0:T(8,128)(2,1)} async-done(((bf16[1,128,2048]{2,1,0:T(8,128)(2,1)}), bf16[1,256,2048]{2,1,0:T(8,128)(2,1)}) %all-gather.5.cloned.1.call-update) | async-done | bytes 1048592 | tf_op jit(solution)/shard_map/all_gather | solution.py:47
  32.9 1.5 collective-permute-start
  34.4 25.3 %collective-permute-done = bf16[1,256,2048]{2,1,0:T(8,128)(2,1)S(1)} collective-permute-done((bf16[1,256,2048]{2,1,0:T(8,128)(2,1)}, bf16[1,256,2048]{2,1,0:T(8,128)(2,1)S(1)}, u32[]{:S(2)}, u32[]{:S(2)}) %collective-permute-start) | collective-permute-done | bytes 1048608 | tf_op jit(solution)/shard_map/ppermute | solution.py:12
  59.7 0.0 copy-start
  59.7 0.0 collective-permute-start.1
  59.7 1.6 fusion.52
  61.2 4.4 %fusion.47 = (f32[]{:T(128)}, f32[]{:T(128)}, f32[]{:T(128)}, f32[]{:T(128)}, f32[]{:T(128)}) fusion(f32[4]{0:T(128)} %param.6, s32[]{:T(128)} %bitcast.32, s32[]{:T(128)} %bitcast.18, s32[]{:T(128)} %bitcast.8, s32[]{:T(128)} %bitcast.7, s32[]{:T(128)} %bitcast.25), kind=kLoop, calls=%fused_computation.61 | loop fusion | flops 55 | bytes 56 | tf_op jit(solution)/shard_map/reduce_sum | solution.py:18
  70.6 0.7 reshape.218
  71.3 0.7 constant_dynamic-slice_fusion.1
  72.0 1.0 select_reduce_fusion
  73.1 12.3 %collective-permute-done.1 = bf16[1,256,2048]{2,1,0:T(8,128)(2,1)S(1)} collective-permute-done((bf16[1,256,2048]{2,1,0:T(8,128)(2,1)S(1)}, bf16[1,256,2048]{2,1,0:T(8,128)(2,1)S(1)}, u32[]{:S(2)}, u32[]{:S(2)}) %collective-permute-start.1) | collective-permute-done | bytes 1048608 | tf_op jit(solution)/shard_map/ppermute | solution.py:12
  85.3 0.0 copy-start.1
  85.3 0.0 all-gather.3.cloned.1.call-done
  85.3 2.7 %fusion.2 = f32[512,256]{1,0:T(8,128)S(1)} fusion(bf16[1,512,2048]{2,1,0:T(8,128)(2,1)} %all-gather.3.cloned.1.call-done, bf16[1,256,2048]{2,1,0:T(8,128)(2,1)S(1)} %collective-permute-done.1), kind=kOutput, calls=%fused_computation.3 | convolution fusion | flops 536870912 | bytes 3670016 | tf_op jit(solution)/shard_map/iap,jbp->iajb/dot_general | solution.py:55
  88.0 0.0 copy-done.1
  88.1 0.3 reshape.225
  88.3 0.8 copy.32
  89.2 3.5 %all-to-all-start.2 = ((f32[8,1,128,1,128]{4,2,3,1,0:T(8,128)}), f32[8,1,128,1,128]{4,2,3,1,0:T(8,128)S(1)}, u32[]{:S(2)}, u32[]{:S(2)}) async-start(f32[8,1,128,1,128]{4,2,3,1,0:T(8,128)} %bitcast.22), calls=%async_computation.2 | async-start | bytes 1048576 | tf_op jit(solution)/shard_map/all_to_all | solution.py:62
  92.7 0.1 collective-permute-start.2
  92.8 0.0 copy-done
  92.8 2.3 %fusion.4 = f32[512,256]{1,0:T(8,128)S(1)} fusion(bf16[1,512,2048]{2,1,0:T(8,128)(2,1)} %all-gather.3.cloned.1.call-done, bf16[1,256,2048]{2,1,0:T(8,128)(2,1)S(1)} %collective-permute-done), kind=kOutput, calls=%fused_computation.5 | convolution fusion | flops 536870912 | bytes 3670016 | tf_op jit(solution)/shard_map/iap,jbp->iajb/dot_general | solution.py:55
  95.1 0.0 copy-start.2
  95.1 0.3 reshape.220
  95.4 0.8 copy.29
  96.2 5.2 %all-to-all-done.2 = f32[8,1,128,1,128]{4,2,3,1,0:T(8,128)S(1)} async-done(((f32[8,1,128,1,128]{4,2,3,1,0:T(8,128)}), f32[8,1,128,1,128]{4,2,3,1,0:T(8,128)S(1)}, u32[]{:S(2)}, u32[]{:S(2)}) %all-to-all-start.2) | async-done | bytes 524320 | tf_op jit(solution)/shard_map/all_to_all | solution.py:62
  101.5 3.5 %all-to-all-start.1 = ((f32[8,1,128,1,128]{4,2,3,1,0:T(8,128)}), f32[8,1,128,1,128]{4,2,3,1,0:T(8,128)S(1)}, u32[]{:S(2)}, u32[]{:S(2)}) async-start(f32[8,1,128,1,128]{4,2,3,1,0:T(8,128)} %bitcast.15), calls=%async_computation.1 | async-start | bytes 1048576 | tf_op jit(solution)/shard_map/all_to_all | solution.py:62
  105.0 0.0 copy-done.2
  105.0 0.2 select_reduce_fusion.1
  105.2 2.6 %fusion.6 = f32[512,256]{1,0:T(8,128)S(1)} fusion(bf16[1,512,2048]{2,1,0:T(8,128)(2,1)} %all-gather.3.cloned.1.call-done, bf16[1,256,2048]{2,1,0:T(8,128)(2,1)} %all-gather.5.cloned.1.call-done), kind=kOutput, calls=%fused_computation.7 | convolution fusion | flops 536870912 | bytes 3670016 | tf_op jit(solution)/shard_map/iap,jbp->iajb/dot_general | solution.py:55
  107.8 0.3 reshape.213
  108.1 0.8 copy.26
  109.0 0.3 copy.34
  109.2 4.5 %all-to-all-done.1 = f32[8,1,128,1,128]{4,2,3,1,0:T(8,128)S(1)} async-done(((f32[8,1,128,1,128]{4,2,3,1,0:T(8,128)}), f32[8,1,128,1,128]{4,2,3,1,0:T(8,128)S(1)}, u32[]{:S(2)}, u32[]{:S(2)}) %all-to-all-start.1) | async-done | bytes 524320 | tf_op jit(solution)/shard_map/all_to_all | solution.py:62
  113.7 3.5 %all-to-all-start = ((f32[8,1,128,1,128]{4,2,3,1,0:T(8,128)}), f32[8,1,128,1,128]{4,2,3,1,0:T(8,128)S(1)}, u32[]{:S(2)}, u32[]{:S(2)}) async-start(f32[8,1,128,1,128]{4,2,3,1,0:T(8,128)} %bitcast.118), calls=%async_computation | async-start | bytes 1048576 | tf_op jit(solution)/shard_map/all_to_all | solution.py:62
  117.2 3.9 %fusion.10 = f32[512,2048]{1,0:T(8,128)} fusion(bf16[1,256,2048]{2,1,0:T(8,128)(2,1)} %copy-done.1, f32[64,8,2,128]{3,2,1,0:T(2,128)S(1)} %bitcast.112, f32[512,256]{1,0:T(8,128)S(1)} %fusion.2, f32[512]{0:T(512)S(1)} %get-tuple-element.11, f32[256]{0:T(256)S(1)} %select_reduce_fusion.1), kind=kOutput, calls=%fused_computation.13 | convolution fusion | flops 537526272 | bytes 6294528 | tf_op jit(solution)/shard_map/iajb,jbp->iap/dot_general | solution.py:76
  121.2 0.3 copy.31
  121.4 0.0 collective-permute-done.2
  121.4 2.6 %fusion = f32[512,256]{1,0:T(8,128)S(1)} fusion(bf16[1,512,2048]{2,1,0:T(8,128)(2,1)} %all-gather.3.cloned.1.call-done, bf16[1,256,2048]{2,1,0:T(8,128)(2,1)} %collective-permute-done.2), kind=kOutput, calls=%fused_computation.1 | convolution fusion | flops 536870912 | bytes 3670016 | tf_op jit(solution)/shard_map/iap,jbp->iajb/dot_general | solution.py:55
  124.0 0.3 reshape.230
  124.3 0.8 copy.35
  125.1 0.9 all-to-all-done
  126.0 3.5 %all-to-all-start.3 = ((f32[8,1,128,1,128]{4,2,3,1,0:T(8,128)}), f32[8,1,128,1,128]{4,2,3,1,0:T(8,128)S(1)}, u32[]{:S(2)}, u32[]{:S(2)}) async-start(f32[8,1,128,1,128]{4,2,3,1,0:T(8,128)} %bitcast.29), calls=%async_computation.3 | async-start | bytes 1048576 | tf_op jit(solution)/shard_map/all_to_all | solution.py:62
  129.5 0.0 reduce-scatter.2.cloned.1.call-start
  129.6 4.0 %fusion.13 = f32[512,2048]{1,0:T(8,128)} fusion(bf16[1,256,2048]{2,1,0:T(8,128)(2,1)} %copy-done, f32[64,8,2,128]{3,2,1,0:T(2,128)S(1)} %bitcast.111, f32[512,256]{1,0:T(8,128)S(1)} %fusion.4, f32[512]{0:T(512)S(1)} %get-tuple-element.12, f32[256]{0:T(256)S(1)} %select_reduce_fusion.1), kind=kOutput, calls=%fused_computation.16 | convolution fusion | flops 537526272 | bytes 6294528 | tf_op jit(solution)/shard_map/iajb,jbp->iap/dot_general | solution.py:76
  133.6 0.3 copy.28
  133.8 4.0 %fusion.16 = f32[512,2048]{1,0:T(8,128)} fusion(bf16[1,256,2048]{2,1,0:T(8,128)(2,1)} %all-gather.5.cloned.1.call-done, f32[64,8,2,128]{3,2,1,0:T(2,128)S(1)} %bitcast.114, f32[512,256]{1,0:T(8,128)S(1)} %fusion.6, f32[256]{0:T(256)S(1)} %select_reduce_fusion.1, f32[512]{0:T(512)S(1)} %get-tuple-element.13), kind=kOutput, calls=%fused_computation.19 | convolution fusion | flops 537526272 | bytes 6294528 | tf_op jit(solution)/shard_map/iajb,jbp->iap/dot_general | solution.py:76
  137.8 0.5 all-to-all-done.3
  138.3 0.3 copy.37
  138.6 7.8 %add_bitcast_fusion = f32[1,512,2048]{2,1,0:T(8,128)} fusion(f32[512,2048]{1,0:T(8,128)} %fusion.10, f32[512,2048]{1,0:T(8,128)} %fusion.16, f32[512,2048]{1,0:T(8,128)} %fusion.13, bf16[1,256,2048]{2,1,0:T(8,128)(2,1)} %collective-permute-done.2, f32[64,8,2,128]{3,2,1,0:T(2,128)S(1)} %bitcast.113, f32[512,256]{1,0:T(8,128)S(1)} %fusion, ...), kind=kOutput, calls=%fused_computation | convolution fusion | flops 540672000 | bytes 18877440 | tf_op jit(solution)/shard_map/iajb,jbp->iap/dot_general | solution.py:76
  146.3 0.0 reduce-scatter.2.cloned.1.call-update
  146.4 42.8 %reduce-scatter.2.cloned.1.call-done = f32[1,128,2048]{2,1,0:T(8,128)} async-done(((f32[1,512,2048]{2,1,0:T(8,128)}), f32[1,128,2048]{2,1,0:T(8,128)}) %reduce-scatter.2.cloned.1.call-update) | async-done | bytes 1048592 | tf_op jit(solution)/shard_map/reduce_scatter | solution.py:79
  (2 shorter events, 0.0 us)
Async XLA Ops:
  6.5 26.4 %all-gather.5.cloned.1.call-start = ((), (), s32[]{:S(2)}) async-start(), calls=%async_computation.6 | async-start | bytes 1572864 | tf_op jit(solution)/shard_map/all_gather | solution.py:47
  7.3 78.1 %all-gather.3.cloned.1.call-start = ((), (), s32[]{:S(2)}) async-start(), calls=%async_computation.5 | async-start | bytes 2621440 | tf_op jit(solution)/shard_map/all_gather | solution.py:48
  32.9 26.7 %collective-permute-start = (bf16[1,256,2048]{2,1,0:T(8,128)(2,1)}, bf16[1,256,2048]{2,1,0:T(8,128)(2,1)S(1)}, u32[]{:S(2)}, u32[]{:S(2)}) collective-permute-start(bf16[1,256,2048]{2,1,0:T(8,128)(2,1)} %all-gather.5.cloned.1.call-done), channel_id=1, source_target_pairs={{24,0},{0,8},{8,16},{16,24},{25,1},{1,9},{9,17},{17,25},{26,2},{2,... | collective-permute-start | bytes 3145736 | tf_op jit(solution)/shard_map/ppermute | solution.py:12
  59.7 33.1 %copy-start = (bf16[1,256,2048]{2,1,0:T(8,128)(2,1)}, bf16[1,256,2048]{2,1,0:T(8,128)(2,1)S(1)}, u32[]{:S(2)}) copy-start(bf16[1,256,2048]{2,1,0:T(8,128)(2,1)S(1)} %collective-permute-done) | copy-start | bytes 3145732
  59.7 25.7 %collective-permute-start.1 = (bf16[1,256,2048]{2,1,0:T(8,128)(2,1)S(1)}, bf16[1,256,2048]{2,1,0:T(8,128)(2,1)S(1)}, u32[]{:S(2)}, u32[]{:S(2)}) collective-permute-start(bf16[1,256,2048]{2,1,0:T(8,128)(2,1)S(1)} %collective-permute-done), channel_id=1, source_target_pairs={{24,0},{0,8},{8,16},{16,24},{25,1},{1,9},{9,17},{17,25},{26,2},{2,... | collective-permute-start | bytes 3145736 | tf_op jit(solution)/shard_map/ppermute | solution.py:12
  85.3 2.7 %copy-start.1 = (bf16[1,256,2048]{2,1,0:T(8,128)(2,1)}, bf16[1,256,2048]{2,1,0:T(8,128)(2,1)S(1)}, u32[]{:S(2)}) copy-start(bf16[1,256,2048]{2,1,0:T(8,128)(2,1)S(1)} %collective-permute-done.1) | copy-start | bytes 3145732
  89.2 12.3 %all-to-all-start.2 = ((f32[8,1,128,1,128]{4,2,3,1,0:T(8,128)}), f32[8,1,128,1,128]{4,2,3,1,0:T(8,128)S(1)}, u32[]{:S(2)}, u32[]{:S(2)}) async-start(f32[8,1,128,1,128]{4,2,3,1,0:T(8,128)} %bitcast.22), calls=%async_computation.2 | async-start | bytes 1048576 | tf_op jit(solution)/shard_map/all_to_all | solution.py:62
  92.7 28.7 %collective-permute-start.2 = (bf16[1,256,2048]{2,1,0:T(8,128)(2,1)}, bf16[1,256,2048]{2,1,0:T(8,128)(2,1)}, u32[]{:S(2)}, u32[]{:S(2)}) collective-permute-start(bf16[1,256,2048]{2,1,0:T(8,128)(2,1)} %copy-done.1), channel_id=1, source_target_pairs={{24,0},{0,8},{8,16},{16,24},{25,1},{1,9},{9,17},{17,25},{26,2},{2,... | collective-permute-start | bytes 3145736 | tf_op jit(solution)/shard_map/ppermute | solution.py:12
  95.1 9.9 %copy-start.2 = (f32[1024]{0:T(1024)S(1)}, f32[1024]{0:T(1024)}, u32[]{:S(2)}) copy-start(f32[1024]{0:T(1024)} %param.7) | copy-start | bytes 12292
  101.5 12.3 %all-to-all-start.1 = ((f32[8,1,128,1,128]{4,2,3,1,0:T(8,128)}), f32[8,1,128,1,128]{4,2,3,1,0:T(8,128)S(1)}, u32[]{:S(2)}, u32[]{:S(2)}) async-start(f32[8,1,128,1,128]{4,2,3,1,0:T(8,128)} %bitcast.15), calls=%async_computation.1 | async-start | bytes 1048576 | tf_op jit(solution)/shard_map/all_to_all | solution.py:62
  113.7 12.3 %all-to-all-start = ((f32[8,1,128,1,128]{4,2,3,1,0:T(8,128)}), f32[8,1,128,1,128]{4,2,3,1,0:T(8,128)S(1)}, u32[]{:S(2)}, u32[]{:S(2)}) async-start(f32[8,1,128,1,128]{4,2,3,1,0:T(8,128)} %bitcast.118), calls=%async_computation | async-start | bytes 1048576 | tf_op jit(solution)/shard_map/all_to_all | solution.py:62
  126.0 12.3 %all-to-all-start.3 = ((f32[8,1,128,1,128]{4,2,3,1,0:T(8,128)}), f32[8,1,128,1,128]{4,2,3,1,0:T(8,128)S(1)}, u32[]{:S(2)}, u32[]{:S(2)}) async-start(f32[8,1,128,1,128]{4,2,3,1,0:T(8,128)} %bitcast.29), calls=%async_computation.3 | async-start | bytes 1048576 | tf_op jit(solution)/shard_map/all_to_all | solution.py:62
  129.5 59.6 %reduce-scatter.2.cloned.1.call-start = ((), (), s32[]{:S(2)}) async-start(), calls=%async_computation.7 | async-start | bytes 5242880 | tf_op jit(solution)/shard_map/reduce_scatter | solution.py:79
Sparse Core Ops, SparseCore 0:
  8.9 23.9 all-gather.4
  34.5 22.5 all-gather.2
  146.5 42.5 reduce-scatter.1
where the time goes:
time: 197 us; the launch traced here: 196 us
  waiting for transfers between devices  118 us (60%)
  matrix products  29.9 us (15%)
  between operations  18.3 us (9%)
  starting transfers between devices  15.6 us (8%)
  local copies, waits for them, and re-layouts  8.41 us (4%)
  other arithmetic  5.74 us (3%)
    reduce_scatter x1, waiting for transfers between devices, per_device(): return lax.psum_scatter(gradient, 'vb', scatter_dimension=1, tiled=True)  42.8 us
    ppermute x3, waiting for transfers between devices, passed_along(): return lax.ppermute(block, axis, route)  37.5 us
    all_gather x1, waiting for transfers between devices, per_device(): own_columns = lax.all_gather(aux_factors, 'va', axis=1, tiled=True)  24.9 us
    dot_general x4, matrix products, per_device(): jnp.einsum('iajb,jbp->iap', weights, far_columns, preferred_element_type=...  19.6 us
    all_to_all x4, starting transfers between devices, per_device(): lax.all_to_all(outgoing, ('va', 'vb'), split_axis=0, concat_axis=0, tiled...  14 us
    all_to_all x4, waiting for transfers between devices, per_device(): lax.all_to_all(outgoing, ('va', 'vb'), split_axis=0, concat_axis=0, tiled...  11.1 us
    dot_general x4, matrix products, per_device(): jnp.einsum('iap,jbp->iajb', own_rows, far_columns, preferred_element_type...  10.2 us
    reduce_sum x3, other arithmetic, lookup(): return jnp.sum(jnp.where(matches, energies[None, :], 0.0), axis=1)  5.73 us
  transfers between devices with their start and end apart: 10, of which 8 were waited for; matrix products, arithmetic and copies ran while one was open for 16% of the time, Pallas kernels for 0%

commit v1 on v0

--- a/solution.py
+++ b/solution.py
@@ -44,7 +44,7 @@
         )
 
     own_energy = block_energy(occ_rank)
-    own_columns = lax.all_gather(aux_factors, "va", axis=1, tiled=True)
+    own_columns = jnp.concatenate(lax.all_gather(aux_factors, "va"), axis=1)
     own_rows = lax.all_gather(aux_factors, "vb", axis=1, tiled=True)
     gradient = jnp.zeros((occ_rows, row_count, aux_width), jnp.float32)
     far_columns = own_columns

time: 197 us -> 187 us (0.949)
  waiting for transfers between devices: 118 us -> 109 us
    all_to_all x4, waiting for transfers between devices: 11.1 us -> 5.03 us  [per_device(): lax.all_to_all(outgoing, ('va', 'vb'), split_axis=0, concat_axis=0, tiled...]
    ppermute x3, waiting for transfers between devices: 37.5 us -> 31.7 us  [passed_along(): return lax.ppermute(block, axis, route)]
    reduce_scatter x1, waiting for transfers between devices: 42.8 us -> 45.5 us  [per_device(): return lax.psum_scatter(gradient, 'vb', scatter_dimension=1, tiled=True)]
  transfers between devices with their start and end apart: 10 -> 10, of which waited for: 8 -> 7; matrix products, arithmetic and copies ran while one was open for 16% -> 19% of each run, Pallas kernels for 0% -> 0%
where the time goes in v1:
time: 187 us
  waiting for transfers between devices  109 us (58%)
  matrix products  30 us (16%)
  between operations  18.3 us (10%)
  starting transfers between devices  15.5 us (8%)
  local copies, waits for them, and re-layouts  8.51 us (5%)
  other arithmetic  5.68 us (3%)
    reduce_scatter x1, waiting for transfers between devices, per_device(): return lax.psum_scatter(gradient, 'vb', scatter_dimension=1, tiled=True)  45.5 us
    ppermute x3, waiting for transfers between devices, passed_along(): return lax.ppermute(block, axis, route)  31.7 us
    all_gather x1, waiting for transfers between devices, per_device(): own_columns = jnp.concatenate(lax.all_gather(aux_factors, 'va'), axis=1)  24.9 us
    dot_general x4, matrix products, per_device(): jnp.einsum('iajb,jbp->iap', weights, far_columns, preferred_element_type=...  19.6 us
    all_to_all x4, starting transfers between devices, per_device(): lax.all_to_all(outgoing, ('va', 'vb'), split_axis=0, concat_axis=0, tiled...  14 us
    dot_general x4, matrix products, per_device(): jnp.einsum('iap,jbp->iajb', own_rows, far_columns, preferred_element_type...  10.4 us
    reduce_sum x3, other arithmetic, lookup(): return jnp.sum(jnp.where(matches, energies[None, :], 0.0), axis=1)  5.67 us
    all_to_all x4, waiting for transfers between devices, per_device(): lax.all_to_all(outgoing, ('va', 'vb'), split_axis=0, concat_axis=0, tiled...  5.03 us
  transfers between devices with their start and end apart: 10, of which 7 were waited for; matrix products, arithmetic and copies ran while one was open for 19% of the time, Pallas kernels for 0%

profile of v1, /device:TPU:0, one launch (start us, length us, event | category | flops | bytes accessed | tf_op | source)
XLA Modules:
  0.0 186.7 jit_solution(12958665771549099180)
XLA Ops:
  6.5 0.0 all-gather.6.cloned.1.call-start
  6.5 0.7 all-gather.6.cloned.1.call-update
  7.3 0.0 all-gather.4.cloned.1.call-start
  7.3 0.7 all-gather.4.cloned.1.call-update
  8.0 24.9 %all-gather.6.cloned.1.call-done = bf16[2,128,2048]{2,1,0:T(8,128)(2,1)} async-done(((bf16[1,128,2048]{2,1,0:T(8,128)(2,1)}), bf16[2,128,2048]{2,1,0:T(8,128)(2,1)}) %all-gather.6.cloned.1.call-update) | async-done | bytes 1048592 | tf_op jit(solution)/shard_map/all_gather | solution.py:47
  32.9 1.5 collective-permute-start
  34.4 25.3 %collective-permute-done = bf16[1,256,2048]{2,1,0:T(8,128)(2,1)S(1)} collective-permute-done((bf16[1,256,2048]{2,1,0:T(8,128)(2,1)}, bf16[1,256,2048]{2,1,0:T(8,128)(2,1)S(1)}, u32[]{:S(2)}, u32[]{:S(2)}) %collective-permute-start) | collective-permute-done | bytes 1048608 | tf_op jit(solution)/shard_map/ppermute | solution.py:12
  59.7 0.0 copy-start
  59.7 0.0 collective-permute-start.1
  59.7 1.5 fusion.50
  61.2 4.4 %fusion.45 = (f32[]{:T(128)}, f32[]{:T(128)}, f32[]{:T(128)}, f32[]{:T(128)}, f32[]{:T(128)}) fusion(f32[4]{0:T(128)} %param.6, s32[]{:T(128)} %bitcast.33, s32[]{:T(128)} %bitcast.19, s32[]{:T(128)} %bitcast.8, s32[]{:T(128)} %bitcast.7, s32[]{:T(128)} %bitcast.26), kind=kLoop, calls=%fused_computation.59 | loop fusion | flops 55 | bytes 56 | tf_op jit(solution)/shard_map/reduce_sum | solution.py:18
  70.6 0.7 reshape.223
  71.3 0.7 constant_dynamic-slice_fusion.1
  72.0 1.0 select_reduce_fusion
  73.1 0.0 all-gather.4.cloned.1.call-done
  73.1 2.6 %fusion.6 = f32[512,256]{1,0:T(8,128)S(1)} fusion(bf16[256,2048]{1,0:T(8,128)(2,1)} %bitcast.120, bf16[1,512,2048]{2,1,0:T(8,128)(2,1)} %all-gather.4.cloned.1.call-done), kind=kOutput, calls=%fused_computation.7 | convolution fusion | flops 536870912 | bytes 3670016 | tf_op jit(solution)/shard_map/iap,jbp->iajb/dot_general | solution.py:55
  75.7 0.0 copy-done
  75.7 0.3 reshape.218
  76.0 0.9 copy.26
  76.9 3.5 %all-to-all-start = ((f32[8,1,128,1,128]{4,2,3,1,0:T(8,128)}), f32[8,1,128,1,128]{4,2,3,1,0:T(8,128)S(1)}, u32[]{:S(2)}, u32[]{:S(2)}) async-start(f32[8,1,128,1,128]{4,2,3,1,0:T(8,128)} %bitcast.4), calls=%async_computation | async-start | bytes 1048576 | tf_op jit(solution)/shard_map/all_to_all | solution.py:62
  80.4 5.0 %collective-permute-done.1 = bf16[1,256,2048]{2,1,0:T(8,128)(2,1)} collective-permute-done((bf16[1,256,2048]{2,1,0:T(8,128)(2,1)S(1)}, bf16[1,256,2048]{2,1,0:T(8,128)(2,1)}, u32[]{:S(2)}, u32[]{:S(2)}) %collective-permute-start.1) | collective-permute-done | bytes 1048608 | tf_op jit(solution)/shard_map/ppermute | solution.py:12
  85.4 0.0 collective-permute-start.2
  85.4 2.6 %fusion.2 = f32[512,256]{1,0:T(8,128)S(1)} fusion(bf16[1,512,2048]{2,1,0:T(8,128)(2,1)} %all-gather.4.cloned.1.call-done, bf16[1,256,2048]{2,1,0:T(8,128)(2,1)} %collective-permute-done.1), kind=kOutput, calls=%fused_computation.3 | convolution fusion | flops 536870912 | bytes 3670016 | tf_op jit(solution)/shard_map/iap,jbp->iajb/dot_general | solution.py:55
  88.0 0.0 copy-start.1
  88.0 0.3 reshape.231
  88.3 0.9 copy.32
  89.2 0.0 all-to-all-done
  89.2 3.5 %all-to-all-start.2 = ((f32[8,1,128,1,128]{4,2,3,1,0:T(8,128)}), f32[8,1,128,1,128]{4,2,3,1,0:T(8,128)S(1)}, u32[]{:S(2)}, u32[]{:S(2)}) async-start(f32[8,1,128,1,128]{4,2,3,1,0:T(8,128)} %bitcast.23), calls=%async_computation.2 | async-start | bytes 1048576 | tf_op jit(solution)/shard_map/all_to_all | solution.py:62
  92.7 0.0 copy-done.1
  92.7 0.2 select_reduce_fusion.1
  93.0 2.6 %fusion.4 = f32[512,256]{1,0:T(8,128)S(1)} fusion(bf16[1,512,2048]{2,1,0:T(8,128)(2,1)} %all-gather.4.cloned.1.call-done, bf16[1,256,2048]{2,1,0:T(8,128)(2,1)} %copy-done), kind=kOutput, calls=%fused_computation.5 | convolution fusion | flops 536870912 | bytes 3670016 | tf_op jit(solution)/shard_map/iap,jbp->iajb/dot_general | solution.py:55
  95.6 0.3 reshape.226
  95.9 0.9 copy.29
  96.8 0.3 copy.28
  97.0 4.5 %all-to-all-done.2 = f32[8,1,128,1,128]{4,2,3,1,0:T(8,128)S(1)} async-done(((f32[8,1,128,1,128]{4,2,3,1,0:T(8,128)}), f32[8,1,128,1,128]{4,2,3,1,0:T(8,128)S(1)}, u32[]{:S(2)}, u32[]{:S(2)}) %all-to-all-start.2) | async-done | bytes 524320 | tf_op jit(solution)/shard_map/all_to_all | solution.py:62
  101.5 3.5 %all-to-all-start.1 = ((f32[8,1,128,1,128]{4,2,3,1,0:T(8,128)}), f32[8,1,128,1,128]{4,2,3,1,0:T(8,128)S(1)}, u32[]{:S(2)}, u32[]{:S(2)}) async-start(f32[8,1,128,1,128]{4,2,3,1,0:T(8,128)} %bitcast.117), calls=%async_computation.1 | async-start | bytes 1048576 | tf_op jit(solution)/shard_map/all_to_all | solution.py:62
  105.0 3.9 %fusion.24 = f32[512,2048]{1,0:T(8,128)} fusion(bf16[256,2048]{1,0:T(8,128)(2,1)} %bitcast.121, f32[64,8,2,128]{3,2,1,0:T(2,128)S(1)} %bitcast.111, f32[512,256]{1,0:T(8,128)S(1)} %fusion.6, f32[256]{0:T(256)S(1)} %select_reduce_fusion.1, f32[512]{0:T(512)S(1)} %get-tuple-element.13), kind=kOutput, calls=%fused_computation.33 | convolution fusion | flops 537526272 | bytes 6294528 | tf_op jit(solution)/shard_map/iajb,jbp->iap/dot_general | solution.py:76
  108.9 0.3 copy.34
  109.2 1.4 collective-permute-done.2
  110.6 2.6 %fusion = f32[512,256]{1,0:T(8,128)S(1)} fusion(bf16[1,512,2048]{2,1,0:T(8,128)(2,1)} %all-gather.4.cloned.1.call-done, bf16[1,256,2048]{2,1,0:T(8,128)(2,1)} %collective-permute-done.2), kind=kOutput, calls=%fused_computation.1 | convolution fusion | flops 536870912 | bytes 3670016 | tf_op jit(solution)/shard_map/iap,jbp->iajb/dot_general | solution.py:55
  113.2 0.3 reshape.236
  113.4 0.8 copy.35
  114.3 0.0 all-to-all-done.1
  114.3 3.5 %all-to-all-start.3 = ((f32[8,1,128,1,128]{4,2,3,1,0:T(8,128)}), f32[8,1,128,1,128]{4,2,3,1,0:T(8,128)S(1)}, u32[]{:S(2)}, u32[]{:S(2)}) async-start(f32[8,1,128,1,128]{4,2,3,1,0:T(8,128)} %bitcast.30), calls=%async_computation.3 | async-start | bytes 1048576 | tf_op jit(solution)/shard_map/all_to_all | solution.py:62
  117.8 0.0 reduce-scatter.2.cloned.1.call-start
  117.8 4.0 %fusion.10 = f32[512,2048]{1,0:T(8,128)} fusion(bf16[1,256,2048]{2,1,0:T(8,128)(2,1)} %collective-permute-done.1, f32[64,8,2,128]{3,2,1,0:T(2,128)S(1)} %bitcast.110, f32[512,256]{1,0:T(8,128)S(1)} %fusion.2, f32[512]{0:T(512)S(1)} %get-tuple-element.11, f32[256]{0:T(256)S(1)} %select_reduce_fusion.1), kind=kOutput, calls=%fused_computation.13 | convolution fusion | flops 537526272 | bytes 6294528 | tf_op jit(solution)/shard_map/iajb,jbp->iap/dot_general | solution.py:76
  121.8 0.3 copy.31
  122.0 4.0 %fusion.13 = f32[512,2048]{1,0:T(8,128)} fusion(bf16[1,256,2048]{2,1,0:T(8,128)(2,1)} %copy-done, f32[64,8,2,128]{3,2,1,0:T(2,128)S(1)} %bitcast.113, f32[512,256]{1,0:T(8,128)S(1)} %fusion.4, f32[512]{0:T(512)S(1)} %get-tuple-element.12, f32[256]{0:T(256)S(1)} %select_reduce_fusion.1), kind=kOutput, calls=%fused_computation.16 | convolution fusion | flops 537526272 | bytes 6294528 | tf_op jit(solution)/shard_map/iajb,jbp->iap/dot_general | solution.py:76
  126.0 0.5 all-to-all-done.3
  126.5 0.3 copy.37
  126.8 7.8 %add_bitcast_fusion = f32[1,512,2048]{2,1,0:T(8,128)} fusion(f32[512,2048]{1,0:T(8,128)} %fusion.10, f32[512,2048]{1,0:T(8,128)} %fusion.24, f32[512,2048]{1,0:T(8,128)} %fusion.13, bf16[1,256,2048]{2,1,0:T(8,128)(2,1)} %collective-permute-done.2, f32[64,8,2,128]{3,2,1,0:T(2,128)S(1)} %bitcast.112, f32[512,256]{1,0:T(8,128)S(1)} %fusion, ...), kind=kOutput, calls=%fused_computation | convolution fusion | flops 540672000 | bytes 18877440 | tf_op jit(solution)/shard_map/iajb,jbp->iap/dot_general | solution.py:76
  134.6 0.0 reduce-scatter.2.cloned.1.call-update
  134.6 45.5 %reduce-scatter.2.cloned.1.call-done = f32[1,128,2048]{2,1,0:T(8,128)} async-done(((f32[1,512,2048]{2,1,0:T(8,128)}), f32[1,128,2048]{2,1,0:T(8,128)}) %reduce-scatter.2.cloned.1.call-update) | async-done | bytes 1048592 | tf_op jit(solution)/shard_map/reduce_scatter | solution.py:79
  (2 shorter events, 0.0 us)
Async XLA Ops:
  6.5 26.4 %all-gather.6.cloned.1.call-start = ((), (), s32[]{:S(2)}) async-start(), calls=%async_computation.7 | async-start | bytes 1572864 | tf_op jit(solution)/shard_map/all_gather | solution.py:47
  7.3 65.8 %all-gather.4.cloned.1.call-start = ((), (), s32[]{:S(2)}) async-start(), calls=%async_computation.5 | async-start | bytes 2621440 | tf_op jit(solution)/shard_map/all_gather | solution.py:48
  32.9 26.7 %collective-permute-start = (bf16[1,256,2048]{2,1,0:T(8,128)(2,1)}, bf16[1,256,2048]{2,1,0:T(8,128)(2,1)S(1)}, u32[]{:S(2)}, u32[]{:S(2)}) collective-permute-start(bf16[1,256,2048]{2,1,0:T(8,128)(2,1)} %bitcast.119), channel_id=1, source_target_pairs={{24,0},{0,8},{8,16},{16,24},{25,1},{1,9},{9,17},{17,25},{26,2},{2,... | collective-permute-start | bytes 3145736 | tf_op jit(solution)/shard_map/ppermute | solution.py:12
  59.7 16.1 %copy-start = (bf16[1,256,2048]{2,1,0:T(8,128)(2,1)}, bf16[1,256,2048]{2,1,0:T(8,128)(2,1)S(1)}, u32[]{:S(2)}) copy-start(bf16[1,256,2048]{2,1,0:T(8,128)(2,1)S(1)} %collective-permute-done) | copy-start | bytes 3145732
  59.7 25.8 %collective-permute-start.1 = (bf16[1,256,2048]{2,1,0:T(8,128)(2,1)S(1)}, bf16[1,256,2048]{2,1,0:T(8,128)(2,1)}, u32[]{:S(2)}, u32[]{:S(2)}) collective-permute-start(bf16[1,256,2048]{2,1,0:T(8,128)(2,1)S(1)} %collective-permute-done), channel_id=1, source_target_pairs={{24,0},{0,8},{8,16},{16,24},{25,1},{1,9},{9,17},{17,25},{26,2},{2,... | collective-permute-start | bytes 3145736 | tf_op jit(solution)/shard_map/ppermute | solution.py:12
  76.9 12.3 %all-to-all-start = ((f32[8,1,128,1,128]{4,2,3,1,0:T(8,128)}), f32[8,1,128,1,128]{4,2,3,1,0:T(8,128)S(1)}, u32[]{:S(2)}, u32[]{:S(2)}) async-start(f32[8,1,128,1,128]{4,2,3,1,0:T(8,128)} %bitcast.4), calls=%async_computation | async-start | bytes 1048576 | tf_op jit(solution)/shard_map/all_to_all | solution.py:62
  85.4 25.1 %collective-permute-start.2 = (bf16[1,256,2048]{2,1,0:T(8,128)(2,1)}, bf16[1,256,2048]{2,1,0:T(8,128)(2,1)}, u32[]{:S(2)}, u32[]{:S(2)}) collective-permute-start(bf16[1,256,2048]{2,1,0:T(8,128)(2,1)} %collective-permute-done.1), channel_id=1, source_target_pairs={{24,0},{0,8},{8,16},{16,24},{25,1},{1,9},{9,17},{17,25},{26,2},{2,... | collective-permute-start | bytes 3145736 | tf_op jit(solution)/shard_map/ppermute | solution.py:12
  88.0 4.7 %copy-start.1 = (f32[1024]{0:T(1024)S(1)}, f32[1024]{0:T(1024)}, u32[]{:S(2)}) copy-start(f32[1024]{0:T(1024)} %param.7) | copy-start | bytes 12292
  89.2 12.3 %all-to-all-start.2 = ((f32[8,1,128,1,128]{4,2,3,1,0:T(8,128)}), f32[8,1,128,1,128]{4,2,3,1,0:T(8,128)S(1)}, u32[]{:S(2)}, u32[]{:S(2)}) async-start(f32[8,1,128,1,128]{4,2,3,1,0:T(8,128)} %bitcast.23), calls=%async_computation.2 | async-start | bytes 1048576 | tf_op jit(solution)/shard_map/all_to_all | solution.py:62
  101.5 12.8 %all-to-all-start.1 = ((f32[8,1,128,1,128]{4,2,3,1,0:T(8,128)}), f32[8,1,128,1,128]{4,2,3,1,0:T(8,128)S(1)}, u32[]{:S(2)}, u32[]{:S(2)}) async-start(f32[8,1,128,1,128]{4,2,3,1,0:T(8,128)} %bitcast.117), calls=%async_computation.1 | async-start | bytes 1048576 | tf_op jit(solution)/shard_map/all_to_all | solution.py:62
  114.3 12.3 %all-to-all-start.3 = ((f32[8,1,128,1,128]{4,2,3,1,0:T(8,128)}), f32[8,1,128,1,128]{4,2,3,1,0:T(8,128)S(1)}, u32[]{:S(2)}, u32[]{:S(2)}) async-start(f32[8,1,128,1,128]{4,2,3,1,0:T(8,128)} %bitcast.30), calls=%async_computation.3 | async-start | bytes 1048576 | tf_op jit(solution)/shard_map/all_to_all | solution.py:62
  117.8 62.4 %reduce-scatter.2.cloned.1.call-start = ((), (), s32[]{:S(2)}) async-start(), calls=%async_computation.6 | async-start | bytes 5242880 | tf_op jit(solution)/shard_map/reduce_scatter | solution.py:79
Sparse Core Ops, SparseCore 0:
  8.9 23.9 all-gather.5
  34.5 22.5 all-gather.3
  134.7 45.3 reduce-scatter.1
